TPU v7x, 128 devices: a whole 4x4x4 slice. The times are simulated.
128 devices in a mesh: ctx: 32 (over x, z, core), head: 4 (over y).
Axes of the slice: x: 4, y: 4, z: 4, core: 2. Of those that a mesh axis runs over, the one named last changes fastest.
Arguments:
- hidden_in: bfloat16 [16384, 7168], P('ctx', 'head'), may hold values from -6 to 6
- gate_weight: bfloat16 [7168, 192], P('head'), may hold values from -0.09375 to 0.09375
- encoded_queries: bfloat16 [16384, 64, 128], P('ctx', 'head'), may hold values from -12 to 12
- encoded_keys: bfloat16 [16384, 4, 128], P('ctx', 'head'), may hold values from -12 to 12
- value_tensor: bfloat16 [16384, 4, 128], P('ctx', 'head'), may hold values from -6 to 6
- comp_key_weight: float32 [64, 128], replicated, may hold values from -0.75 to 0.75
- comp_value_weight: float32 [64, 128], replicated, may hold values from -0.75 to 0.75
- selection: int32 [256, 4, 16], P('ctx', 'head'), may hold values from 0 to 255, as said below
Outputs:
- attended: bfloat16 [16384, 64, 128], P('ctx', 'head')
Inputs may be any that keep to these rules, and one draw needn't show every extreme that they name: `selection`: entries of one list are distinct and the first is the query block's own block. For one index of ctx and one group, the blocks named over all its query blocks that lie in one other index's shard are at most 4, and some index reaches 4 in every draw.
All inputs are finite; a program needn't handle non-finite values.
Results may differ from a plain program's by a relative error of at most 0.011.
Values may be sent and summed in bfloat16 or wider, within the bound.
No kernel may reach another device: no remote copies, remote signals or barrier semaphores. Data moves between devices by JAX's collectives and lax.ppermute only.
A program may use at most 64 MiB of HBM per device.

v0:
```python
import jax
import jax.numpy as jnp
from jax import lax
from jax.sharding import PartitionSpec as P

WINDOW_TOKENS = 512


def shifted(value, axis, steps):
    count = lax.axis_size(axis)
    initial, last = (max(0, -steps), min(count, count - steps))
    return lax.ppermute(value, axis, [(source, source + steps) for source in range(initial, last)])


def attend(query_block_index, key_rows, value_rows, key_mask, with_null):
    scale = query_block_index.shape[-1] ** (-0.5)
    if key_rows.dtype == jnp.float32:
        scores = (
            jnp.einsum(
                "tgjd,gkd->tgjk",
                query_block_index.astype(jnp.float32),
                key_rows,
                preferred_element_type=jnp.float32,
                precision=lax.Precision.HIGHEST,
            )
            * scale
        )
    else:
        scores = (
            jnp.einsum(
                "tgjd,gkd->tgjk", query_block_index, key_rows, preferred_element_type=jnp.float32
            )
            * scale
        )
    scores = jnp.where(key_mask[:, :, None, :], scores, -1e30)
    peak = jnp.max(scores, axis=-1, keepdims=True)
    if with_null:
        peak = jnp.maximum(peak, 0.0)
    weights = jnp.exp(scores - peak)
    total_w = jnp.sum(weights, axis=-1, keepdims=True)
    if with_null:
        total_w = total_w + jnp.exp(-peak)
    rounded = (weights / total_w).astype(jnp.bfloat16)
    if value_rows.dtype == jnp.float32:
        return jnp.einsum(
            "tgjk,gkd->tgjd",
            rounded.astype(jnp.float32),
            value_rows,
            preferred_element_type=jnp.float32,
            precision=lax.Precision.HIGHEST,
        )
    return jnp.einsum("tgjk,gkd->tgjd", rounded, value_rows, preferred_element_type=jnp.float32)


def body(
    hidden_in,
    gate_weight,
    encoded_queries,
    encoded_keys,
    value_tensor,
    comp_key_weight,
    comp_value_weight,
    selection,
):
    rows_here, heads_here, head_dim = encoded_queries.shape
    block_len = comp_key_weight.shape[0]
    top_count = selection.shape[-1]
    blocks_here = rows_here // block_len
    shard_parts = lax.axis_size("ctx")
    own_index = lax.axis_index("ctx")
    block_count_total = blocks_here * shard_parts
    window_len = WINDOW_TOKENS
    partial_value = jnp.dot(hidden_in, gate_weight, preferred_element_type=jnp.float32)
    logits = lax.psum_scatter(partial_value, "head", scatter_dimension=1, tiled=True)
    gate_values = jax.nn.sigmoid(logits).reshape(rows_here, 1, heads_here, 3)
    key_value = jnp.concatenate([encoded_keys, value_tensor], axis=-1).reshape(
        rows_here, 2 * head_dim
    )
    widened = key_value.astype(jnp.float32).reshape(blocks_here, block_len, 2 * head_dim)
    compress_w = jnp.concatenate([comp_key_weight, comp_value_weight], axis=-1)
    summary = jnp.sum(widened * compress_w[None, :, :], axis=1)
    summaries = lax.all_gather(summary, "ctx", axis=0, tiled=True)
    previous = shifted(key_value, "ctx", 1)
    extended = jnp.concatenate([previous, key_value], axis=0)
    blocks = key_value.reshape(blocks_here, block_len, 2 * head_dim)
    chosen_blocks = selection[:, 0, :]
    all_ids = jnp.arange(block_count_total, dtype=jnp.int32)
    all_blocks = lax.all_gather(blocks, "ctx", axis=0, tiled=True)
    picked = jnp.take(all_blocks, chosen_blocks, axis=0)
    offset = own_index * rows_here
    comp_ends = (all_ids + 1) * block_len - 1
    inner_result = jnp.arange(block_len, dtype=jnp.int32)
    comp_keys = summaries[None, :, :head_dim]
    comp_values = summaries[None, :, head_dim:]

    def per_block(block_num):
        query_start = block_num * block_len
        query_block_index = lax.dynamic_slice_in_dim(
            encoded_queries, query_start, block_len, 0
        ).reshape(block_len, 1, heads_here, head_dim)
        query_pos = offset + query_start + inner_result
        comp_mask = (comp_ends[None, :] <= query_pos[:, None])[:, None, :]
        out_comp = attend(query_block_index, comp_keys, comp_values, comp_mask, True)
        sel_tiles = lax.dynamic_index_in_dim(picked, block_num, 0, keepdims=False).reshape(
            top_count * block_len, 2 * head_dim
        )
        sel_ids = lax.dynamic_index_in_dim(chosen_blocks, block_num, 0, keepdims=False)
        selected_positions = (sel_ids[:, None] * block_len + inner_result[None, :]).reshape(-1)
        sel_mask = (selected_positions[None, :] <= query_pos[:, None])[:, None, :]
        out_sel = attend(
            query_block_index,
            sel_tiles[None, :, :head_dim],
            sel_tiles[None, :, head_dim:],
            sel_mask,
            False,
        )
        win_rows = lax.dynamic_slice_in_dim(extended, query_start, window_len + block_len, 0)
        win_pos = (
            offset + query_start - window_len + jnp.arange(window_len + block_len, dtype=jnp.int32)
        )
        win_mask = (
            (win_pos[None, :] <= query_pos[:, None])
            & (win_pos[None, :] > query_pos[:, None] - window_len)
            & (win_pos[None, :] >= 0)
        )
        out_win = attend(
            query_block_index,
            win_rows[None, :, :head_dim],
            win_rows[None, :, head_dim:],
            win_mask[:, None, :],
            False,
        )
        gate_block_rows = lax.dynamic_slice_in_dim(gate_values, query_start, block_len, 0)
        merged = (
            gate_block_rows[..., 0:1] * out_comp
            + gate_block_rows[..., 1:2] * out_sel
            + gate_block_rows[..., 2:3] * out_win
        )
        return merged.reshape(block_len, heads_here, head_dim).astype(jnp.bfloat16)

    results = lax.map(per_block, jnp.arange(blocks_here, dtype=jnp.int32))
    return results.reshape(rows_here, heads_here, head_dim)


def solution(mesh):
    return jax.shard_map(
        body,
        mesh=mesh,
        in_specs=(
            P("ctx", "head"),
            P("head", None),
            P("ctx", "head", None),
            P("ctx", "head", None),
            P("ctx", "head", None),
            P(),
            P(),
            P("ctx", "head", None),
        ),
        out_specs=P("ctx", "head", None),
        check_vma=False,
    )
```

profile of v0, /device:TPU:1, one launch (start us, length us, event | category | flops | bytes accessed | tf_op | source)
XLA Modules:
  0.0 289.9 jit_solution(7371172152859489917)
XLA Ops:
  8.9 2.6 fusion.55
  12.4 4.9 %collective-permute-start = (bf16[512,256]{1,0:T(8,128)(2,1)}, bf16[512,256]{1,0:T(8,128)(2,1)S(1)}, u32[]{:S(2)}, u32[]{:S(2)}) collective-permute-start(bf16[512,256]{1,0:T(8,128)(2,1)} %bitcast.175), channel_id=1, source_target_pairs={{0,4},{4,8},{8,12},{12,16},{16,20},{20,24},{24,28},{28,32},{32,36}... | collective-permute-start | bytes 786440 | tf_op jit(solution)/shard_map/ppermute | solution.py:12
  18.5 24.4 %all_gather.6 = f32[256,256]{1,0:T(8,128)S(1)} all-gather(f32[8,256]{1,0:T(8,128)S(1)} %multiply_reduce_fusion), channel_id=1, replica_groups=mesh['ctx'=32,'head'=4] {'ctx'}, dimensions={0}, use_global_device_ids=true | all-gather | bytes 270336 | tf_op jit(solution)/shard_map/all_gather | solution.py:82
  47.2 24.0 %all-gather.2.cloned.1.call-done = bf16[256,64,256]{2,1,0:T(8,128)(2,1)} async-done(((bf16[8,64,256]{2,1,0:T(8,128)(2,1)}), bf16[256,64,256]{2,1,0:T(8,128)(2,1)}) %all-gather.2.cloned.1.call-update) | async-done | bytes 8388624 | tf_op jit(solution)/shard_map/all_gather | solution.py:88
  71.2 6.2 %gather_fusion = bf16[128,64,256]{2,1,0:T(8,128)(2,1)} fusion(bf16[256,64,256]{2,1,0:T(8,128)(2,1)} %all-gather.2.cloned.1.call-done, s32[1024]{0:T(1024)S(1)} %pad_clamp_fusion), kind=kCustom, calls=%fused_computation | custom fusion | bytes 8389120 | tf_op jit(solution)/shard_map/jit(_take)/gather | solution.py:89
  77.4 4.6 %broadcast_select_fusion = bf16[8,16,64,256]{3,2,1,0:T(8,128)(2,1)} fusion(bf16[8,16,64,256]{3,2,1,0:T(8,128)(2,1)} %bitcast.173, pred[8,16]{1,0:T(8,128)(4,1)S(1)} %compare_and_fusion), kind=kLoop, calls=%fused_computation.68 | loop fusion | flops 2097152 | bytes 8388736 | tf_op jit(solution)/shard_map/jit(_take)/select_n | solution.py:89
  81.9 200.5 %while.15 = (s32[]{:T(128)}, bf16[8,64,16,128]{3,2,1,0:T(8,128)(2,1)}, s32[8]{0:T(128)S(1)}, f32[512,1,16,3]{0,3,2,1:T(4,128)}, s32[]{:T(128)}, /*index=5*/bf16[...) while((s32[]{:T(128)}, ...), condition=%wide.region_9.10_spmd.clone.clone, body=%wide.region_2.9_spmd.clone.clone.sunk | while | flops 1666942592 | bytes 35800808 | solution.py:141
  92.5 3.7 %fusion.85 = f32[1,128,64,16]{1,3,2,0:T(8,128)} fusion(bf16[64,16,1024]{2,0,1:T(8,128)(2,1)} %fusion.84, bf16[1024,256]{1,0:T(8,128)(2,1)S(1)} %bitcast.172, f32[64,16]{1,0:T(8,128)S(1)} %bitcast.180), kind=kOutput, calls=%fused_computation.23.clone.1 | convolution fusion | flops 268566528 | bytes 2916352 | tf_op jit(solution)/shard_map/while/body/eval_jaxpr/tgjk,gkd->tgjd/dot_general | solution.py:52
  98.3 2.7 fusion.88
  104.2 2.8 fusion.92
  117.5 3.7 %fusion.85 = f32[1,128,64,16]{1,3,2,0:T(8,128)} fusion(bf16[64,16,1024]{2,0,1:T(8,128)(2,1)} %fusion.84, bf16[1024,256]{1,0:T(8,128)(2,1)S(1)} %bitcast.172, f32[64,16]{1,0:T(8,128)S(1)} %bitcast.180), kind=kOutput, calls=%fused_computation.23.clone.1 | convolution fusion | flops 268566528 | bytes 2916352 | tf_op jit(solution)/shard_map/while/body/eval_jaxpr/tgjk,gkd->tgjd/dot_general | solution.py:52
  123.4 2.7 fusion.88
  129.3 2.8 fusion.92
  142.6 3.7 %fusion.85 = f32[1,128,64,16]{1,3,2,0:T(8,128)} fusion(bf16[64,16,1024]{2,0,1:T(8,128)(2,1)} %fusion.84, bf16[1024,256]{1,0:T(8,128)(2,1)S(1)} %bitcast.172, f32[64,16]{1,0:T(8,128)S(1)} %bitcast.180), kind=kOutput, calls=%fused_computation.23.clone.1 | convolution fusion | flops 268566528 | bytes 2916352 | tf_op jit(solution)/shard_map/while/body/eval_jaxpr/tgjk,gkd->tgjd/dot_general | solution.py:52
  148.4 2.7 fusion.88
  154.4 2.8 fusion.92
  164.5 2.1 fusion.84
  167.7 3.7 %fusion.85 = f32[1,128,64,16]{1,3,2,0:T(8,128)} fusion(bf16[64,16,1024]{2,0,1:T(8,128)(2,1)} %fusion.84, bf16[1024,256]{1,0:T(8,128)(2,1)S(1)} %bitcast.172, f32[64,16]{1,0:T(8,128)S(1)} %bitcast.180), kind=kOutput, calls=%fused_computation.23.clone.1 | convolution fusion | flops 268566528 | bytes 2916352 | tf_op jit(solution)/shard_map/while/body/eval_jaxpr/tgjk,gkd->tgjd/dot_general | solution.py:52
  173.5 2.7 fusion.88
  179.4 2.8 fusion.92
  192.7 3.7 %fusion.85 = f32[1,128,64,16]{1,3,2,0:T(8,128)} fusion(bf16[64,16,1024]{2,0,1:T(8,128)(2,1)} %fusion.84, bf16[1024,256]{1,0:T(8,128)(2,1)S(1)} %bitcast.172, f32[64,16]{1,0:T(8,128)S(1)} %bitcast.180), kind=kOutput, calls=%fused_computation.23.clone.1 | convolution fusion | flops 268566528 | bytes 2916352 | tf_op jit(solution)/shard_map/while/body/eval_jaxpr/tgjk,gkd->tgjd/dot_general | solution.py:52
  198.5 2.7 fusion.88
  204.5 2.8 fusion.92
  217.8 3.7 %fusion.85 = f32[1,128,64,16]{1,3,2,0:T(8,128)} fusion(bf16[64,16,1024]{2,0,1:T(8,128)(2,1)} %fusion.84, bf16[1024,256]{1,0:T(8,128)(2,1)S(1)} %bitcast.172, f32[64,16]{1,0:T(8,128)S(1)} %bitcast.180), kind=kOutput, calls=%fused_computation.23.clone.1 | convolution fusion | flops 268566528 | bytes 2916352 | tf_op jit(solution)/shard_map/while/body/eval_jaxpr/tgjk,gkd->tgjd/dot_general | solution.py:52
  223.6 2.7 fusion.88
  229.5 2.8 fusion.92
  242.8 3.7 %fusion.85 = f32[1,128,64,16]{1,3,2,0:T(8,128)} fusion(bf16[64,16,1024]{2,0,1:T(8,128)(2,1)} %fusion.84, bf16[1024,256]{1,0:T(8,128)(2,1)S(1)} %bitcast.172, f32[64,16]{1,0:T(8,128)S(1)} %bitcast.180), kind=kOutput, calls=%fused_computation.23.clone.1 | convolution fusion | flops 268566528 | bytes 2916352 | tf_op jit(solution)/shard_map/while/body/eval_jaxpr/tgjk,gkd->tgjd/dot_general | solution.py:52
  248.7 2.7 fusion.88
  254.6 2.8 fusion.92
  267.9 3.7 %fusion.85 = f32[1,128,64,16]{1,3,2,0:T(8,128)} fusion(bf16[64,16,1024]{2,0,1:T(8,128)(2,1)} %fusion.84, bf16[1024,256]{1,0:T(8,128)(2,1)S(1)} %bitcast.172, f32[64,16]{1,0:T(8,128)S(1)} %bitcast.180), kind=kOutput, calls=%fused_computation.23.clone.1 | convolution fusion | flops 268566528 | bytes 2916352 | tf_op jit(solution)/shard_map/while/body/eval_jaxpr/tgjk,gkd->tgjd/dot_general | solution.py:52
  273.7 2.7 fusion.88
  279.7 2.8 fusion.92
  (249 shorter events, 112.5 us)
Async XLA Ops:
  7.4 1.5 copy-start
  7.4 4.2 %copy-start.2 = (bf16[512,1,128]{2,0,1:T(8,128)(2,1)S(1)}, bf16[512,1,128]{2,0,1:T(8,128)(2,1)}, u32[]{:S(2)}) copy-start(bf16[512,1,128]{2,0,1:T(8,128)(2,1)} %param.13) | copy-start | bytes 393220
  7.4 4.2 %copy-start.3 = (bf16[512,1,128]{2,0,1:T(8,128)(2,1)S(1)}, bf16[512,1,128]{2,0,1:T(8,128)(2,1)}, u32[]{:S(2)}) copy-start(bf16[512,1,128]{2,0,1:T(8,128)(2,1)} %param.14) | copy-start | bytes 393220
  7.4 10.0 %copy-start.6 = (s32[8,1,16]{2,1,0:T(1,128)S(1)}, s32[8,1,16]{2,1,0:T(1,128)}, u32[]{:S(2)}) copy-start(s32[8,1,16]{2,1,0:T(1,128)} %param.17) | copy-start | bytes 1540
  7.4 10.1 %copy-start.4 = (f32[64,128]{1,0:T(8,128)S(1)}, f32[64,128]{1,0:T(8,128)}, u32[]{:S(2)}) copy-start(f32[64,128]{1,0:T(8,128)} %param.16) | copy-start | bytes 98308
  7.4 10.1 %copy-start.5 = (f32[64,128]{1,0:T(8,128)S(1)}, f32[64,128]{1,0:T(8,128)}, u32[]{:S(2)}) copy-start(f32[64,128]{1,0:T(8,128)} %param.15) | copy-start | bytes 98308
  7.4 38.1 %reduce-scatter.2.cloned.1.call-start = ((), (), s32[]{:S(2)}) async-start(), calls=%async_computation.1 | async-start | bytes 491520 | tf_op jit(solution)/shard_map/reduce_scatter | solution.py:74
  11.5 59.7 %all-gather.2.cloned.1.call-start = ((), (), s32[]{:S(2)}) async-start(), calls=%async_computation.2 | async-start | bytes 8650752 | tf_op jit(solution)/shard_map/all_gather | solution.py:88
  11.7 0.7 copy-start.1
  12.4 31.3 %collective-permute-start = (bf16[512,256]{1,0:T(8,128)(2,1)}, bf16[512,256]{1,0:T(8,128)(2,1)S(1)}, u32[]{:S(2)}, u32[]{:S(2)}) collective-permute-start(bf16[512,256]{1,0:T(8,128)(2,1)} %bitcast.175), channel_id=1, source_target_pairs={{0,4},{4,8},{8,12},{12,16},{16,20},{20,24},{24,28},{28,32},{32,36}... | collective-permute-start | bytes 786440 | tf_op jit(solution)/shard_map/ppermute | solution.py:12
Sparse Core Ops, SparseCore 0:
  11.6 22.3 reduce-scatter.1
Sparse Core Ops, SparseCore 1:
  14.5 56.6 all-gather.1
where the time goes:
time: 293 us; the launch traced here: 290 us
  matrix products  108 us (37%)
  other arithmetic  51.1 us (17%)
  local copies, waits for them, and re-layouts  41.5 us (14%)
  blocking collectives  24.4 us (8%)
  waiting for transfers between devices  24.1 us (8%)
  loops' own time  20.8 us (7%)
  between operations  15 us (5%)
  starting transfers between devices  5.02 us (2%)
    dot_general x16, matrix products, attend(): jnp.einsum('tgjk,gkd->tgjd', rounded, value_rows, preferred_element_type=...  51.4 us
    all_gather x1, blocking collectives, body(): summaries = lax.all_gather(summary, 'ctx', axis=0, tiled=True)  24.4 us
    all_gather x1, waiting for transfers between devices, body(): all_blocks = lax.all_gather(blocks, 'ctx', axis=0, tiled=True)  24 us
    another operation x16, other arithmetic  21.9 us
    dot_general x8, matrix products, attend(): jnp.einsum('tgjk,gkd->tgjd', rounded.astype(jnp.float32), value_rows, pre...  21.3 us
    another operation x1, loops' own time, body(): results = lax.map(per_block, jnp.arange(blocks_here, dtype=jnp.int32))  20.8 us
    dot_general x16, matrix products, attend(): jnp.einsum('tgjd,gkd->tgjk', query_block_index, key_rows, preferred_eleme...  20 us
    reduce_sum x24, other arithmetic, attend(): total_w = jnp.sum(weights, axis=-1, keepdims=True)  17.6 us
  transfers between devices with their start and end apart: 3, of which 1 were waited for; matrix products, arithmetic and copies ran while one was open for 2% of the time, Pallas kernels for 0%

commit v1 on v0

--- a/solution.py
+++ b/solution.py
@@ -85,7 +85,9 @@
     blocks = key_value.reshape(blocks_here, block_len, 2 * head_dim)
     chosen_blocks = selection[:, 0, :]
     all_ids = jnp.arange(block_count_total, dtype=jnp.int32)
-    all_blocks = lax.all_gather(blocks, "ctx", axis=0, tiled=True)
+    all_blocks = jnp.concatenate(
+        lax.all_to_all(jnp.stack([blocks] * lax.axis_size("ctx")), "ctx", 0, 0), axis=0
+    )
     picked = jnp.take(all_blocks, chosen_blocks, axis=0)
     offset = own_index * rows_here
     comp_ends = (all_ids + 1) * block_len - 1

time: 293 us -> 378 us (1.29)
  blocking collectives: 24.4 us -> 134 us
  waiting for transfers between devices: 24.1 us -> 0.04 us
  matrix products: 108 us -> 95.3 us
  starting transfers between devices: 5.02 us -> 13.2 us
  other arithmetic: 51.1 us -> 57.2 us
    all_gather x1, blocking collectives: 24.4 us -> 134 us  [body(): summaries = lax.all_gather(summary, 'ctx', axis=0, tiled=True)]
    all_gather x1 -> x0, waiting for transfers between devices: 24 us -> none  [body(): all_blocks = lax.all_gather(blocks, 'ctx', axis=0, tiled=True)]
    all_to_all x0 -> x1, starting transfers between devices: none -> 9.62 us  [body(): lax.all_to_all(jnp.stack([blocks] * lax.axis_size('ctx')), 'ctx', 0, 0)]
    another operation x16, other arithmetic: 21.9 us -> 30.6 us
    dot_general x8, matrix products: 12.6 us -> 5.34 us  [attend(): jnp.einsum('tgjd,gkd->tgjk', query_block_index.astype(jnp.float32), key_r...]
    dot_general x16, matrix products: 20 us -> 12.7 us  [attend(): jnp.einsum('tgjd,gkd->tgjk', query_block_index, key_rows, preferred_eleme...]
    slice x8, local copies, waits for them, and re-layouts: 7.86 us -> 0.93 us  [per_block(): gate_block_rows[..., 2:3] * out_win]
    another operation x0 -> x1, local copies, waits for them, and re-layouts: none -> 4.28 us  [body(): jnp.stack([blocks] * lax.axis_size('ctx'))]
  transfers between devices with their start and end apart: 3 -> 3, of which waited for: 1 -> 0; matrix products, arithmetic and copies ran while one was open for 2% -> 1% of each run, Pallas kernels for 0% -> 0%
where the time goes in v1:
time: 378 us; the launch traced here: 374 us
  blocking collectives  134 us (35%)
  matrix products  95.3 us (25%)
  other arithmetic  57.2 us (15%)
  local copies, waits for them, and re-layouts  38.5 us (10%)
  loops' own time  22.9 us (6%)
  between operations  13.6 us (4%)
  starting transfers between devices  13.2 us (3%)
    all_gather x1, blocking collectives, body(): summaries = lax.all_gather(summary, 'ctx', axis=0, tiled=True)  134 us
    dot_general x16, matrix products, attend(): jnp.einsum('tgjk,gkd->tgjd', rounded, value_rows, preferred_element_type=...  54.8 us
    another operation x16, other arithmetic  30.6 us
    another operation x1, loops' own time, body(): results = lax.map(per_block, jnp.arange(blocks_here, dtype=jnp.int32))  22.9 us
    dot_general x8, matrix products, attend(): jnp.einsum('tgjk,gkd->tgjd', rounded.astype(jnp.float32), value_rows, pre...  21 us
    reduce_sum x24, other arithmetic, attend(): total_w = jnp.sum(weights, axis=-1, keepdims=True)  17.6 us
    dot_general x16, matrix products, attend(): jnp.einsum('tgjd,gkd->tgjk', query_block_index, key_rows, preferred_eleme...  12.7 us
    all_to_all x1, starting transfers between devices, body(): lax.all_to_all(jnp.stack([blocks] * lax.axis_size('ctx')), 'ctx', 0, 0)  9.62 us
  transfers between devices with their start and end apart: 3, of which 0 were waited for; matrix products, arithmetic and copies ran while one was open for 1% of the time, Pallas kernels for 0%

profile of v1, /device:TPU:1, one launch (start us, length us, event | category | flops | bytes accessed | tf_op | source)
XLA Modules:
  0.0 374.4 jit_solution(9893987944380831838)
XLA Ops:
  8.5 4.3 %stack.3 = bf16[32,8,64,256]{3,2,1,0:T(8,128)(2,1)} broadcast(bf16[8,64,256]{2,1,0:T(8,128)(2,1)S(1)} %bitcast.175), dimensions={1,2,3} | broadcast | bytes 8650752 | tf_op jit(solution)/shard_map/stack | solution.py:89
  12.8 9.6 %all-to-all-start = ((bf16[32,8,64,256]{3,2,1,0:T(8,128)(2,1)}), bf16[32,8,64,256]{3,2,1,0:T(8,128)(2,1)}, u32[]{:S(2)}, u32[]{:S(2)}) async-start(bf16[32,8,64,256]{3,2,1,0:T(8,128)(2,1)} %stack.3), calls=%async_computation.1 | async-start | bytes 16777216 | tf_op jit(solution)/shard_map/all_to_all | solution.py:89
  22.5 3.5 collective-permute-start
  27.8 133.7 %all_gather.3 = f32[256,256]{1,0:T(8,128)S(1)} all-gather(f32[8,256]{1,0:T(8,128)S(1)} %multiply_reduce_fusion), channel_id=1, replica_groups=mesh['ctx'=32,'head'=4] {'ctx'}, dimensions={0}, use_global_device_ids=true | all-gather | bytes 270336 | tf_op jit(solution)/shard_map/all_gather | solution.py:82
  162.6 6.2 %gather_fusion = bf16[128,64,256]{2,1,0:T(8,128)(2,1)} fusion(bf16[256,64,256]{2,1,0:T(8,128)(2,1)} %bitcast.4, s32[1024]{0:T(1024)S(1)} %pad_clamp_fusion), kind=kCustom, calls=%fused_computation | custom fusion | bytes 8389120 | tf_op jit(solution)/shard_map/jit(_take)/gather | solution.py:91
  168.8 4.6 %broadcast_select_fusion = bf16[8,16,64,256]{3,2,1,0:T(8,128)(2,1)} fusion(bf16[8,16,64,256]{3,2,1,0:T(8,128)(2,1)} %bitcast.174, pred[8,16]{1,0:T(8,128)(4,1)S(1)} %compare_and_fusion), kind=kLoop, calls=%fused_computation.68 | loop fusion | flops 2097152 | bytes 8388736 | tf_op jit(solution)/shard_map/jit(_take)/select_n | solution.py:91
  173.3 194.2 %while.15 = (s32[]{:T(128)}, bf16[8,64,16,128]{3,2,1,0:T(8,128)(2,1)}, s32[8]{0:T(128)S(1)}, f32[512,1,16,3]{0,3,2,1:T(4,128)S(1)}, s32[]{:T(128)}, /*index=5*/b...) while((s32[]{:T(128)}, ...), condition=%wide.region_9.10_spmd.clone.clone, body=%wide.region_2.9_spmd.clone.clone.sunk | while | flops 1666942592 | bytes 40133232 | solution.py:143
  184.5 2.1 fusion.84
  186.8 3.7 fusion.85
  191.7 2.6 fusion.88
  194.4 3.1 fusion.92
  211.1 3.7 fusion.85
  216.0 2.6 fusion.88
  218.7 3.1 fusion.92
  235.3 3.7 fusion.85
  240.3 2.6 fusion.88
  243.0 3.1 fusion.92
  259.6 3.7 fusion.85
  264.6 2.6 fusion.88
  267.3 3.1 fusion.92
  283.9 3.7 fusion.85
  288.9 2.6 fusion.88
  291.6 3.1 fusion.92
  308.2 3.7 fusion.85
  313.1 2.6 fusion.88
  315.9 3.1 fusion.92
  332.5 3.7 fusion.85
  337.4 2.6 fusion.88
  340.1 3.1 fusion.92
  356.7 3.7 fusion.85
  361.7 2.6 fusion.88
  364.4 3.1 fusion.92
  (325 shorter events, 98.2 us)
Async XLA Ops:
  6.5 19.5 %copy-start = (bf16[512,1792]{1,0:T(8,128)(2,1)S(1)}, bf16[512,1792]{1,0:T(8,128)(2,1)}, u32[]{:S(2)}) copy-start(bf16[512,1792]{1,0:T(8,128)(2,1)} %param.10) | copy-start | bytes 5505028
  12.8 13.3 %copy-start.3 = (bf16[1792,192]{0,1:T(8,128)(2,1)S(1)}, bf16[1792,192]{0,1:T(8,128)(2,1)}, u32[]{:S(2)}) copy-start(bf16[1792,192]{0,1:T(8,128)(2,1)} %param.11) | copy-start | bytes 2064388
  12.8 149.8 %all-to-all-start = ((bf16[32,8,64,256]{3,2,1,0:T(8,128)(2,1)}), bf16[32,8,64,256]{3,2,1,0:T(8,128)(2,1)}, u32[]{:S(2)}, u32[]{:S(2)}) async-start(bf16[32,8,64,256]{3,2,1,0:T(8,128)(2,1)} %stack.3), calls=%async_computation.1 | async-start | bytes 16777216 | tf_op jit(solution)/shard_map/all_to_all | solution.py:89
  22.4 5.2 %copy-start.6 = (s32[8,1,16]{2,1,0:T(1,128)S(1)}, s32[8,1,16]{2,1,0:T(1,128)}, u32[]{:S(2)}) copy-start(s32[8,1,16]{2,1,0:T(1,128)} %param.17) | copy-start | bytes 1540
  22.5 5.3 %copy-start.4 = (f32[64,128]{1,0:T(8,128)S(1)}, f32[64,128]{1,0:T(8,128)}, u32[]{:S(2)}) copy-start(f32[64,128]{1,0:T(8,128)} %param.16) | copy-start | bytes 98308
  22.5 5.2 %copy-start.5 = (f32[64,128]{1,0:T(8,128)S(1)}, f32[64,128]{1,0:T(8,128)}, u32[]{:S(2)}) copy-start(f32[64,128]{1,0:T(8,128)} %param.15) | copy-start | bytes 98308
  22.5 139.1 %reduce-scatter.2.cloned.1.call-start = ((), (), s32[]{:S(2)}) async-start(), calls=%async_computation.2 | async-start | bytes 491520 | tf_op jit(solution)/shard_map/reduce_scatter | solution.py:74
  22.5 139.0 %collective-permute-start = (bf16[512,256]{1,0:T(8,128)(2,1)S(1)}, bf16[512,256]{1,0:T(8,128)(2,1)S(1)}, u32[]{:S(2)}, u32[]{:S(2)}) collective-permute-start(bf16[512,256]{1,0:T(8,128)(2,1)S(1)} %bitcast.176), channel_id=1, source_target_pairs={{0,4},{4,8},{8,12},{12,16},{16,20},{20,24},{24,28},{28,32},{32,36}... | collective-permute-start | bytes 786440 | tf_op jit(solution)/shard_map/ppermute | solution.py:12
  173.4 4.0 %copy-start.1 = (bf16[1024,256]{1,0:T(8,128)(2,1)}, bf16[1024,256]{1,0:T(8,128)(2,1)S(1)}, u32[]{:S(2)}) copy-start(bf16[1024,256]{1,0:T(8,128)(2,1)S(1)} %get-tuple-element.455) | copy-start | bytes 1572868 | tf_op jit(solution)/shard_map/while
  194.4 3.2 copy-start.2
  194.4 3.2 copy-start.7
  194.4 3.2 copy-start.9
  197.6 4.0 %copy-start.1 = (bf16[1024,256]{1,0:T(8,128)(2,1)}, bf16[1024,256]{1,0:T(8,128)(2,1)S(1)}, u32[]{:S(2)}) copy-start(bf16[1024,256]{1,0:T(8,128)(2,1)S(1)} %get-tuple-element.455) | copy-start | bytes 1572868 | tf_op jit(solution)/shard_map/while
  218.6 3.2 copy-start.2
  218.6 3.2 copy-start.7
  218.6 3.2 copy-start.9
  221.9 4.0 %copy-start.1 = (bf16[1024,256]{1,0:T(8,128)(2,1)}, bf16[1024,256]{1,0:T(8,128)(2,1)S(1)}, u32[]{:S(2)}) copy-start(bf16[1024,256]{1,0:T(8,128)(2,1)S(1)} %get-tuple-element.455) | copy-start | bytes 1572868 | tf_op jit(solution)/shard_map/while
  242.9 3.2 copy-start.9
  246.2 4.0 %copy-start.1 = (bf16[1024,256]{1,0:T(8,128)(2,1)}, bf16[1024,256]{1,0:T(8,128)(2,1)S(1)}, u32[]{:S(2)}) copy-start(bf16[1024,256]{1,0:T(8,128)(2,1)S(1)} %get-tuple-element.455) | copy-start | bytes 1572868 | tf_op jit(solution)/shard_map/while
  267.2 3.2 copy-start.7
  267.2 3.2 copy-start.9
  270.5 4.0 %copy-start.1 = (bf16[1024,256]{1,0:T(8,128)(2,1)}, bf16[1024,256]{1,0:T(8,128)(2,1)S(1)}, u32[]{:S(2)}) copy-start(bf16[1024,256]{1,0:T(8,128)(2,1)S(1)} %get-tuple-element.455) | copy-start | bytes 1572868 | tf_op jit(solution)/shard_map/while
  291.5 3.2 copy-start.7
  291.5 3.2 copy-start.9
  294.7 4.0 %copy-start.1 = (bf16[1024,256]{1,0:T(8,128)(2,1)}, bf16[1024,256]{1,0:T(8,128)(2,1)S(1)}, u32[]{:S(2)}) copy-start(bf16[1024,256]{1,0:T(8,128)(2,1)S(1)} %get-tuple-element.455) | copy-start | bytes 1572868 | tf_op jit(solution)/shard_map/while
  315.8 3.2 copy-start.9
  319.0 4.0 %copy-start.1 = (bf16[1024,256]{1,0:T(8,128)(2,1)}, bf16[1024,256]{1,0:T(8,128)(2,1)S(1)}, u32[]{:S(2)}) copy-start(bf16[1024,256]{1,0:T(8,128)(2,1)S(1)} %get-tuple-element.455) | copy-start | bytes 1572868 | tf_op jit(solution)/shard_map/while
  340.0 3.2 copy-start.7
  340.0 3.2 copy-start.9
  343.3 4.0 %copy-start.1 = (bf16[1024,256]{1,0:T(8,128)(2,1)}, bf16[1024,256]{1,0:T(8,128)(2,1)S(1)}, u32[]{:S(2)}) copy-start(bf16[1024,256]{1,0:T(8,128)(2,1)S(1)} %get-tuple-element.455) | copy-start | bytes 1572868 | tf_op jit(solution)/shard_map/while
  364.3 3.2 copy-start.7
  364.3 3.2 copy-start.9
  (16 other events, 37.2 us)
Sparse Core Ops, SparseCore 0:
  27.7 19.9 reduce-scatter.1
